TPU v7x, 32 devices: a whole 2x2x4 slice. The times are simulated.
32 devices in a mesh: band: 8 (over z, y), tok: 4 (over x, core).
Axes of the slice: x: 2, y: 2, z: 4, core: 2. Of those that a mesh axis runs over, the one named last changes fastest.
Arguments:
- pixels: bfloat16 [4, 8, 32, 256, 256], P('tok', None, 'band'), may hold values from -6 to 6
- wave_table: float32 [64], replicated, may hold values from 0.4 to 12
- wave_index: int32 [4, 8, 32], P('tok'), may hold values from 0 to 63
- patch_count: int32 [4, 8], P('tok', 'band'), may hold values from 49 to 256, as said below
- d_out: bfloat16 [4, 8, 256, 768], P('tok', 'band'), may hold values from -6 to 6
- gen_w: bfloat16 [196608, 128], P(('band', 'tok')), may hold values from -0.5 to 0.5
- gen_b: float32 [128, 768], replicated, may hold values from -0.25 to 0.25
- bias_token: float32 [128], replicated, may hold values from -6 to 6
- hyper_query: float32 [128, 128], replicated, may hold values from -1 to 1
- hyper_key: float32 [128, 128], replicated, may hold values from -1 to 1
- hyper_value: float32 [128, 128], replicated, may hold values from -0.5 to 0.5
- hyper_out: float32 [128, 128], replicated, may hold values from -0.5 to 0.5
- hyper_up: float32 [128, 2048], replicated, may hold values from -0.5 to 0.5
- hyper_down: float32 [2048, 128], replicated, may hold values from -0.125 to 0.125
- hyper_gain1: float32 [128], replicated, may hold values from 0.1 to 1.9
- hyper_gain2: float32 [128], replicated, may hold values from 0.1 to 1.9
- w_qkv: bfloat16 [768, 2304], P(None, 'tok'), may hold values from -0.21875 to 0.21875
- w_out: bfloat16 [768, 768], P(None, 'tok'), may hold values from -1.75 to 1.75
- w_up: bfloat16 [768, 3072], P(None, 'tok'), may hold values from -0.21875 to 0.21875
- w_down: bfloat16 [3072, 768], P('tok'), may hold values from -0.109375 to 0.109375
- ln1_gain: float32 [768], replicated, may hold values from 0.5 to 1.5
- ln2_gain: float32 [768], replicated, may hold values from 0.5 to 1.5
Outputs:
- layer_out: bfloat16 [4, 8, 256, 768], P('tok', 'band')
- pixel_grad: bfloat16 [4, 8, 32, 256, 256], P('tok', None, 'band')
- grad_gen_w: float32 [196608, 128], P(('band', 'tok'))
- grad_gen_b: float32 [128, 768], replicated
- grad_bias_token: float32 [128], replicated
- grad_hyper_query: float32 [128, 128], replicated
- grad_hyper_key: float32 [128, 128], replicated
- grad_hyper_value: float32 [128, 128], replicated
- grad_hyper_out: float32 [128, 128], replicated
- grad_hyper_up: float32 [128, 2048], replicated
- grad_hyper_down: float32 [2048, 128], replicated
- grad_hyper_gain1: float32 [128], replicated
- grad_hyper_gain2: float32 [128], replicated
- grad_w_qkv: float32 [768, 2304], P(None, ('band', 'tok'))
- grad_w_out: float32 [768, 768], P(None, ('band', 'tok'))
- grad_w_up: float32 [768, 3072], P(None, ('band', 'tok'))
- grad_w_down: float32 [3072, 768], P(('band', 'tok'))
- grad_ln1_gain: float32 [768], P(('band', 'tok'))
- grad_ln2_gain: float32 [768], P(('band', 'tok'))
Inputs may be any that keep to these rules, and one draw needn't show every extreme that they name: `patch_count`: each entry is 49, 196 or 256; every draw has an image with 49 and one with 256.
All inputs are finite; a program needn't handle non-finite values.
Results may differ from a plain program's by a relative error of at most 0.028.
Values may be sent and summed in bfloat16 or wider, within the bound.
A program may use at most 384 MiB of HBM per device.

v0:
```python
import math
import jax
import jax.numpy as jnp
from jax import lax
from jax.sharding import PartitionSpec as P

HD = 64
HHEADS = 4
EPS_BLOCK = 1e-06
EPS_HYPER = 1e-05
PRECISE = lax.Precision.HIGHEST


def layer_norm(values, scaling, epsilon):
    center = values - jnp.mean(values, axis=-1, keepdims=True)
    spread = jnp.mean(center * center, axis=-1, keepdims=True)
    return center * lax.rsqrt(spread + epsilon) * scaling


def block_norm(values, scaling):
    return layer_norm(values, scaling, EPS_BLOCK)


def exact_gelu(values):
    return jax.nn.gelu(values, approximate=False)


def wave_features(lengths, model_dim):
    middle = model_dim // 2
    angular = 1.0 / 10000.0 ** (jnp.arange(middle, dtype=jnp.float32) / middle)
    phases = (100.0 * lengths)[..., None] * angular
    return jnp.concatenate([jnp.sin(phases), jnp.cos(phases)], axis=-1)


def hyper_layer(features, params):
    (
        bias_token,
        hyper_query,
        hyper_key,
        hyper_value,
        hyper_out,
        hyper_up,
        hyper_down,
        hyper_gain1,
        hyper_gain2,
    ) = params
    images = features.shape[0]
    model_dim = features.shape[-1]
    head_size = model_dim // HHEADS
    tokens = jnp.concatenate(
        [features, jnp.broadcast_to(bias_token, (images, 1, model_dim))], axis=1
    )
    length = tokens.shape[1]
    queries = jnp.einsum("nsc,ce->nse", tokens, hyper_query, precision=PRECISE).reshape(
        images, length, HHEADS, head_size
    )
    keys_all = jnp.einsum("nsc,ce->nse", tokens, hyper_key, precision=PRECISE).reshape(
        images, length, HHEADS, head_size
    )
    values_all = jnp.einsum("nsc,ce->nse", tokens, hyper_value, precision=PRECISE).reshape(
        images, length, HHEADS, head_size
    )
    scores = jnp.einsum("nshe,nthe->nhst", queries, keys_all, precision=PRECISE) / math.sqrt(
        head_size
    )
    weights = jax.nn.softmax(scores, axis=-1)
    blended = jnp.einsum("nhst,nthe->nshe", weights, values_all, precision=PRECISE).reshape(
        images, length, model_dim
    )
    segment_one = layer_norm(
        tokens + jnp.einsum("nse,ef->nsf", blended, hyper_out, precision=PRECISE),
        hyper_gain1,
        EPS_HYPER,
    )
    expanded = jax.nn.gelu(
        jnp.einsum("nse,ef->nsf", segment_one, hyper_up, precision=PRECISE), approximate=False
    )
    second = layer_norm(
        segment_one + jnp.einsum("nsf,fe->nse", expanded, hyper_down, precision=PRECISE),
        hyper_gain2,
        EPS_HYPER,
    )
    return (second[:, :-1, :], second[:, -1, :])


def contract_rows(left_side, right_side):
    return lax.dot_general(
        left_side, right_side, (((0,), (0,)), ((), ())), preferred_element_type=jnp.float32
    )


def contract_cols(left_side, right_side):
    return lax.dot_general(
        left_side, right_side, (((1,), (1,)), ((), ())), preferred_element_type=jnp.float32
    )


def attention_scores(queries, keys_low, usable):
    head_size = queries.shape[-1]
    scores = jnp.einsum(
        "iqhe,ikhe->ihqk", queries, keys_low, preferred_element_type=jnp.float32
    ) / math.sqrt(head_size)
    return jnp.where(usable[:, None, None, :], scores, -1e30)


def block_forward(embedded, usable, weights_full, ln1_gain, ln2_gain):
    w_qkv_full, w_out_full, w_up_full, w_down_full = weights_full
    images, slot_count, model_dim = embedded.shape
    row_count = images * slot_count
    head_count = model_dim // HD
    flat_rows = embedded.reshape(row_count, model_dim)
    normed_one = block_norm(flat_rows, ln1_gain).astype(jnp.bfloat16)
    qkv_low = jnp.dot(normed_one, w_qkv_full, preferred_element_type=jnp.float32).astype(
        jnp.bfloat16
    )
    sections = qkv_low.reshape(images, slot_count, 3, head_count, HD)
    queries = sections[:, :, 0]
    keys_low = sections[:, :, 1]
    values_low = sections[:, :, 2]
    scores = attention_scores(queries, keys_low, usable)
    highest = jnp.max(scores, axis=-1, keepdims=True)
    lifted = jnp.exp(scores - highest)
    totals = jnp.sum(lifted, axis=-1, keepdims=True)
    attn_probs = (lifted / totals).astype(jnp.bfloat16)
    log_mass = highest + jnp.log(totals)
    attended = (
        jnp.einsum("ihqk,ikhe->iqhe", attn_probs, values_low, preferred_element_type=jnp.float32)
        .astype(jnp.bfloat16)
        .reshape(row_count, model_dim)
    )
    middle = flat_rows + jnp.dot(attended, w_out_full, preferred_element_type=jnp.float32)
    normed_two = block_norm(middle, ln2_gain).astype(jnp.bfloat16)
    hidden = jnp.dot(normed_two, w_up_full, preferred_element_type=jnp.float32)
    active = exact_gelu(hidden).astype(jnp.bfloat16)
    output = middle + jnp.dot(active, w_down_full, preferred_element_type=jnp.float32)
    return (
        flat_rows,
        normed_one,
        queries,
        keys_low,
        values_low,
        log_mass,
        attended,
        middle,
        normed_two,
        hidden,
        active,
        output,
    )


def block_backward(stored, usable, grad_rows, weights_full, ln1_gain, ln2_gain):
    (
        flat_rows,
        normed_one,
        queries,
        keys_low,
        values_low,
        log_mass,
        attended,
        middle,
        normed_two,
        hidden,
        active,
        output,
    ) = stored
    w_qkv_full, w_out_full, w_up_full, w_down_full = weights_full
    images, slot_count, head_count, head_size = queries.shape
    row_count, model_dim = flat_rows.shape
    grad_low = grad_rows.astype(jnp.bfloat16)
    grad_down = contract_rows(active, grad_low)
    d_active = contract_cols(grad_low, w_down_full)
    gelu_back = jax.vjp(exact_gelu, hidden)[1]
    d_hidden = gelu_back(d_active)[0].astype(jnp.bfloat16)
    grad_up_turned = contract_rows(d_hidden, normed_two)
    d_normed_two = contract_cols(d_hidden, w_up_full)
    norm_back_two = jax.vjp(block_norm, middle, ln2_gain)[1]
    d_middle_norm, grad_gain_two = norm_back_two(d_normed_two)
    d_middle = grad_rows + d_middle_norm
    d_middle_low = d_middle.astype(jnp.bfloat16)
    grad_out_turned = contract_rows(d_middle_low, attended)
    d_attended = (
        contract_cols(d_middle_low, w_out_full)
        .astype(jnp.bfloat16)
        .reshape(images, slot_count, head_count, head_size)
    )
    scores = attention_scores(queries, keys_low, usable)
    attn_float = jnp.exp(scores - log_mass)
    attn_probs = attn_float.astype(jnp.bfloat16)
    d_values = jnp.einsum(
        "ihqk,iqhe->ikhe", attn_probs, d_attended, preferred_element_type=jnp.float32
    ).astype(jnp.bfloat16)
    d_probs = jnp.einsum(
        "iqhe,ikhe->ihqk", d_attended, values_low, preferred_element_type=jnp.float32
    )
    d_scores = (
        attn_float * (d_probs - jnp.sum(attn_float * d_probs, axis=-1, keepdims=True))
    ).astype(jnp.bfloat16)
    d_queries = (
        jnp.einsum("ihqk,ikhe->iqhe", d_scores, keys_low, preferred_element_type=jnp.float32)
        / math.sqrt(head_size)
    ).astype(jnp.bfloat16)
    d_keys = (
        jnp.einsum("ihqk,iqhe->ikhe", d_scores, queries, preferred_element_type=jnp.float32)
        / math.sqrt(head_size)
    ).astype(jnp.bfloat16)
    d_qkv = jnp.stack([d_queries, d_keys, d_values], axis=2).reshape(row_count, 3 * model_dim)
    grad_qkv_turned = contract_rows(d_qkv, normed_one)
    d_normed_one = contract_cols(d_qkv, w_qkv_full)
    norm_back_one = jax.vjp(block_norm, flat_rows, ln1_gain)[1]
    d_flat, grad_gain_one = norm_back_one(d_normed_one)
    return (
        d_middle + d_flat,
        (grad_qkv_turned, grad_out_turned, grad_up_turned, grad_down, grad_gain_one, grad_gain_two),
    )


def body(
    pixels,
    wave_table,
    wave_index,
    patch_count,
    d_out,
    gen_w,
    gen_b,
    bias_token,
    hyper_query,
    hyper_key,
    hyper_value,
    hyper_out,
    hyper_up,
    hyper_down,
    hyper_gain1,
    hyper_gain2,
    w_qkv,
    w_out,
    w_up,
    w_down,
    ln1_gain,
    ln2_gain,
):
    group_images = pixels.shape[1]
    band_share = pixels.shape[2]
    slot_count = pixels.shape[3]
    pixel_count = pixels.shape[4]
    own_images = patch_count.shape[1]
    model_dim = w_out.shape[0]
    hyper_dim = gen_w.shape[1]
    all_bands = wave_index.shape[2]
    factor = 1.0 / math.sqrt(all_bands * pixel_count)
    band_place = lax.axis_index("band")
    hyper_params = (
        bias_token,
        hyper_query,
        hyper_key,
        hyper_value,
        hyper_out,
        hyper_up,
        hyper_down,
        hyper_gain1,
        hyper_gain2,
    )
    catalog = lax.broadcasted_iota(jnp.int32, (1, 1, wave_table.shape[0]), 2)
    picked = (wave_index[0][:, :, None] == catalog).astype(jnp.float32)
    lengths_all = jnp.sum(picked * wave_table, axis=-1)
    weights_full = (
        lax.all_gather(w_qkv, "tok", axis=1, tiled=True),
        lax.all_gather(w_out, "tok", axis=1, tiled=True),
        lax.all_gather(w_up, "tok", axis=1, tiled=True),
        lax.all_gather(w_down, "tok", axis=0, tiled=True),
    )
    hyper_input = wave_features(lengths_all, hyper_dim)

    def run_hyper(params):
        return hyper_layer(hyper_input, params)

    (band_feats, bias_feats), hyper_back = jax.vjp(run_hyper, hyper_params)
    band_low = (
        lax.dynamic_slice_in_dim(band_feats, band_place * band_share, band_share, 1)
        .astype(jnp.bfloat16)
        .reshape(-1, hyper_dim)
    )
    bias_own = lax.dynamic_slice_in_dim(bias_feats, band_place * own_images, own_images, 0)
    gen_full = lax.all_gather(gen_w, ("band", "tok"), axis=0, tiled=True)
    kernels = (contract_cols(band_low, gen_full) * factor).astype(jnp.bfloat16)
    kernel_grid = kernels.reshape(group_images, band_share, pixel_count, model_dim)
    pixel_part = pixels[0]
    product = jnp.einsum(
        "ibsp,ibpd->isd", pixel_part, kernel_grid, preferred_element_type=jnp.float32
    )
    convolved = lax.psum_scatter(
        product.reshape(own_images * slot_count * lax.axis_size("band"), model_dim).astype(
            jnp.bfloat16
        ),
        "band",
        scatter_dimension=0,
        tiled=True,
    ).astype(jnp.float32)
    bias_rows = jnp.dot(bias_own, gen_b, precision=PRECISE)
    embedded = convolved.reshape(own_images, slot_count, model_dim) + bias_rows[:, None, :]
    usable = lax.broadcasted_iota(jnp.int32, (own_images, slot_count), 1) < patch_count[0][:, None]
    stored = block_forward(embedded, usable, weights_full, ln1_gain, ln2_gain)
    row_mask = usable.reshape(-1, 1)
    layer_out = (
        jnp.where(row_mask, stored[-1], 0.0)
        .astype(jnp.bfloat16)
        .reshape(1, own_images, slot_count, model_dim)
    )
    stored = block_forward(
        lax.optimization_barrier(embedded), usable, weights_full, ln1_gain, ln2_gain
    )
    grad_rows = jnp.where(row_mask, d_out[0].reshape(-1, model_dim).astype(jnp.float32), 0.0)
    d_embed, block_terms = block_backward(
        stored, usable, grad_rows, weights_full, ln1_gain, ln2_gain
    )
    d_embed_low = d_embed.astype(jnp.bfloat16).reshape(own_images, slot_count, model_dim)
    d_bias = jnp.sum(d_embed.reshape(own_images, slot_count, model_dim), axis=1)
    d_bias_feat = jnp.dot(d_bias, gen_b.T, precision=PRECISE)
    grad_gen_b = jnp.dot(bias_own.T, d_bias, precision=PRECISE)
    d_gathered = lax.all_gather(d_embed_low, "band", axis=0, tiled=True)
    pixel_grad = jnp.einsum(
        "isd,ibpd->ibsp", d_gathered, kernel_grid, preferred_element_type=jnp.float32
    ).astype(jnp.bfloat16)[None]
    d_kernel = (
        jnp.einsum("ibsp,isd->ibpd", pixels[0], d_gathered, preferred_element_type=jnp.float32)
        .astype(jnp.bfloat16)
        .reshape(-1, pixel_count * model_dim)
    )
    d_band_local = jnp.dot(d_kernel, gen_full, preferred_element_type=jnp.float32) * factor
    grad_gen_w = lax.psum_scatter(
        contract_rows(d_kernel, band_low) * factor, ("band", "tok"), scatter_dimension=0, tiled=True
    )
    d_band_own = d_band_local.reshape(group_images, band_share, hyper_dim)
    d_band = lax.dynamic_update_slice_in_dim(
        jnp.zeros(band_feats.shape, jnp.float32), d_band_own, band_place * band_share, 1
    )
    d_bias_all = lax.dynamic_update_slice_in_dim(
        jnp.zeros(bias_feats.shape, jnp.float32), d_bias_feat, band_place * own_images, 0
    )
    (
        grad_token,
        grad_query,
        grad_key,
        grad_value,
        grad_mix,
        grad_expand,
        grad_shrink,
        grad_first_gain,
        grad_second_gain,
    ) = hyper_back((d_band, d_bias_all))[0]
    qkv_turned, out_turned, up_turned, grad_down, gain_one, gain_two = block_terms
    block_sums = (
        lax.psum_scatter(qkv_turned, ("band", "tok"), scatter_dimension=0, tiled=True),
        lax.psum_scatter(out_turned, ("band", "tok"), scatter_dimension=0, tiled=True),
        lax.psum_scatter(up_turned, ("band", "tok"), scatter_dimension=0, tiled=True),
        lax.psum_scatter(grad_down, ("band", "tok"), scatter_dimension=0, tiled=True),
        lax.psum_scatter(gain_one, ("band", "tok"), scatter_dimension=0, tiled=True),
        lax.psum_scatter(gain_two, ("band", "tok"), scatter_dimension=0, tiled=True),
    )
    hyper_sums = lax.psum(
        (
            grad_token,
            grad_query,
            grad_key,
            grad_value,
            grad_mix,
            grad_expand,
            grad_shrink,
            grad_first_gain,
            grad_second_gain,
            grad_gen_b,
        ),
        ("band", "tok"),
    )
    return (
        layer_out,
        pixel_grad,
        grad_gen_w,
        hyper_sums[9],
        hyper_sums[0],
        hyper_sums[1],
        hyper_sums[2],
        hyper_sums[3],
        hyper_sums[4],
        hyper_sums[5],
        hyper_sums[6],
        hyper_sums[7],
        hyper_sums[8],
        block_sums[0].T,
        block_sums[1].T,
        block_sums[2].T,
        block_sums[3],
        block_sums[4],
        block_sums[5],
    )


def solution(mesh):
    placed = (
        P("tok", None, "band", None, None),
        P(),
        P("tok", None, None),
        P("tok", "band"),
        P("tok", "band", None, None),
        P(("band", "tok"), None),
        P(),
        P(),
        P(),
        P(),
        P(),
        P(),
        P(),
        P(),
        P(),
        P(),
        P(None, "tok"),
        P(None, "tok"),
        P(None, "tok"),
        P("tok", None),
        P(),
        P(),
    )
    return jax.shard_map(
        body,
        mesh=mesh,
        in_specs=placed,
        out_specs=(
            P("tok", "band", None, None),
            P("tok", None, "band", None, None),
            P(("band", "tok"), None),
            P(),
            P(),
            P(),
            P(),
            P(),
            P(),
            P(),
            P(),
            P(),
            P(),
            P(None, ("band", "tok")),
            P(None, ("band", "tok")),
            P(None, ("band", "tok")),
            P(("band", "tok"), None),
            P(("band", "tok")),
            P(("band", "tok")),
        ),
        check_vma=False,
    )
```

profile of v0, /device:TPU:0, one launch (start us, length us, event | category | flops | bytes accessed | tf_op | source)
XLA Modules:
  0.0 2059.1 jit_solution(18307944858478254983)
XLA Ops:
  21.3 6.0 fusion.22
  30.2 259.9 %all-gather.8.cloned.1.call-done = bf16[196608,128]{1,0:T(8,128)(2,1)} async-done(((bf16[6144,128]{1,0:T(8,128)(2,1)}), bf16[196608,128]{1,0:T(8,128)(2,1)}) %all-gather.8.cloned.1.call-update) | async-done | bytes 50331664 | tf_op jit(solution)/shard_map/all_gather | solution.py:284
  290.0 25.9 %fusion.1 = bf16[32,196608]{1,0:T(8,128)(2,1)} fusion(bf16[32,128]{1,0:T(8,128)(2,1)S(1)} %bitcast.310, bf16[196608,128]{1,0:T(8,128)(2,1)} %all-gather.8.cloned.1.call-done), kind=kOutput, calls=%fused_computation.3 | convolution fusion | flops 1623195648 | bytes 62922752 | tf_op jit(solution)/shard_map/dot_general | solution.py:93
  315.9 8.2 copy.211
  333.5 69.1 %reduce-scatter.7.cloned.1.call-done = bf16[256,768]{1,0:T(8,128)(2,1)} async-done(((bf16[2048,768]{1,0:T(8,128)(2,1)}), bf16[256,768]{1,0:T(8,128)(2,1)}) %reduce-scatter.7.cloned.1.call-update) | async-done | bytes 393232 | tf_op jit(solution)/shard_map/reduce_scatter | solution.py:291
  427.7 29.5 %all-gather.16.cloned.1.call-done = bf16[3072,768]{1,0:T(8,128)(2,1)} async-done(((bf16[768,768]{1,0:T(8,128)(2,1)}), bf16[3072,768]{1,0:T(8,128)(2,1)}) %all-gather.16.cloned.1.call-update) | async-done | bytes 4718608 | tf_op jit(solution)/shard_map/all_gather | solution.py:270
  457.3 10.8 add_convert_fusion
  495.9 51.9 %all-gather.18.cloned.1.call-done = bf16[2048,768]{1,0:T(8,128)(2,1)} async-done(((bf16[256,768]{1,0:T(8,128)(2,1)}), bf16[2048,768]{1,0:T(8,128)(2,1)}) %all-gather.18.cloned.1.call-update) | async-done | bytes 3145744 | tf_op jit(solution)/shard_map/all_gather | solution.py:320
  547.8 11.1 convert_bitcast_fusion
  558.8 16.8 copy.212
  575.6 23.0 %convolution_multiply_fusion.5 = f32[32,128]{1,0:T(8,128)S(1)} fusion(bf16[32,196608]{1,0:T(8,128)(2,1)} %bitcast.272, bf16[196608,128]{1,0:T(8,128)(2,1)} %all-gather.8.cloned.1.call-done), kind=kOutput, calls=%fused_computation.123 | convolution fusion | flops 1610616832 | bytes 62930944 | tf_op jit(solution)/shard_map/dot_general | solution.py:329
  628.8 6.3 convolution_bitcast_fusion
  641.6 11.6 fusion.34
  653.9 6.6 fusion.194
  661.3 39.6 %convolution_multiply_fusion = f32[196608,128]{1,0:T(8,128)} fusion(bf16[32,196608]{1,0:T(8,128)(2,1)} %bitcast.273, bf16[32,128]{1,0:T(8,128)(2,1)S(1)} %bitcast.311), kind=kOutput, calls=%fused_computation.1 | convolution fusion | flops 1635778560 | bytes 113254400 | tf_op jit(solution)/shard_map/dot_general | solution.py:87
  710.2 13.5 fusion.65
  723.7 11.1 convert_bitcast_fusion.1
  734.9 6.6 copy.179
  745.3 39.6 %all-reduce.4 = (f32[128]{0:T(128)}, f32[128]{0:T(128)}, f32[128]{0:T(128)}, f32[768]{0:T(1024)S(1)}, f32[768]{0:T(1024)S(1)}) all-reduce(f32[128]{0:T(128)S(1)} %fusion.148, f32[128]{0:T(128)S(1)} %copy-done.107, f32[128]{0:T(128)S(1)} %copy-done.106, f32[768]{0:T(1024)S(1)} %copy-done.105, ...), channel_id=1, replica_groups=mesh['band'=8,'tok'=4] {'band','tok'}, use_global_device_ids=true, to_apply=%region_34.35 | all-reduce | flops 1920 | bytes 15360 | tf_op jit(solution)/shard_map/psum | solution.py:360
  786.1 12.8 all-reduce.8.cloned.1.call-done
  798.9 124.6 %reduce-scatter.11.cloned.1.call-done = f32[72,768]{1,0:T(8,128)} async-done(((f32[2304,768]{1,0:T(8,128)}), f32[72,768]{1,0:T(8,128)}) %reduce-scatter.11.cloned.1.call-update) | async-done | bytes 221200 | tf_op jit(solution)/shard_map/reduce_scatter | solution.py:353
  923.5 142.3 %reduce-scatter.17.cloned.1.call-done = f32[96,768]{1,0:T(8,128)} async-done(((f32[3072,768]{1,0:T(8,128)}), f32[96,768]{1,0:T(8,128)}) %reduce-scatter.17.cloned.1.call-update) | async-done | bytes 294928 | tf_op jit(solution)/shard_map/reduce_scatter | solution.py:356
  1065.8 141.0 %reduce-scatter.15.cloned.1.call-done = f32[96,768]{1,0:T(8,128)} async-done(((f32[3072,768]{1,0:T(8,128)}), f32[96,768]{1,0:T(8,128)}) %reduce-scatter.15.cloned.1.call-update) | async-done | bytes 294928 | tf_op jit(solution)/shard_map/reduce_scatter | solution.py:355
  1206.8 833.8 %reduce-scatter.9.cloned.1.call-done = f32[6144,128]{1,0:T(8,128)} async-done(((f32[196608,128]{1,0:T(8,128)}), f32[6144,128]{1,0:T(8,128)}) %reduce-scatter.9.cloned.1.call-update) | async-done | bytes 3145744 | tf_op jit(solution)/shard_map/reduce_scatter | solution.py:330
  (373 shorter events, 139.6 us)
Async XLA Ops:
  8.1 282.0 %all-gather.8.cloned.1.call-start = ((), (), s32[]{:S(2)}) async-start(), calls=%async_computation.6 | async-start | bytes 51904512 | tf_op jit(solution)/shard_map/all_gather | solution.py:284
  8.8 393.8 %reduce-scatter.7.cloned.1.call-start = ((), (), s32[]{:S(2)}) async-start(), calls=%async_computation.7 | async-start | bytes 3538944 | tf_op jit(solution)/shard_map/reduce_scatter | solution.py:291
  29.9 286.0 %copy-start.67 = (f32[8,33]{1,0:T(8,128)}, f32[8,33]{1,0:T(8,128)S(1)}, u32[]{:S(2)}) copy-start(f32[8,33]{1,0:T(8,128)S(1)} %multiply_reduce_fusion.14) | copy-start | bytes 3172
  30.2 285.8 %copy-start.57 = (bf16[8,4,128]{2,1,0:T(4,128)(2,1)}, bf16[8,4,128]{2,1,0:T(4,128)(2,1)S(1)}, u32[]{:S(2)}) copy-start(bf16[8,4,128]{2,1,0:T(4,128)(2,1)S(1)} %dynamic-slice_convert_fusion) | copy-start | bytes 24580
  329.9 76.1 %all-gather.10.cloned.1.call-start = ((), (), s32[]{:S(2)}) async-start(), calls=%async_computation.8 | async-start | bytes 4423680 | tf_op jit(solution)/shard_map/all_gather | solution.py:267
  330.5 75.6 %copy-start.69 = (f32[768]{0:T(1024)S(1)}, f32[768]{0:T(1024)}, u32[]{:S(2)}) copy-start(f32[768]{0:T(1024)} %param.42) | copy-start | bytes 9220
  330.5 88.0 %all-gather.12.cloned.1.call-start = ((), (), s32[]{:S(2)}) async-start(), calls=%async_computation.9 | async-start | bytes 1474560 | tf_op jit(solution)/shard_map/all_gather | solution.py:268
  331.1 91.2 %all-gather.14.cloned.1.call-start = ((), (), s32[]{:S(2)}) async-start(), calls=%async_computation.10 | async-start | bytes 5898240 | tf_op jit(solution)/shard_map/all_gather | solution.py:269
  331.6 125.6 %all-gather.16.cloned.1.call-start = ((), (), s32[]{:S(2)}) async-start(), calls=%async_computation.11 | async-start | bytes 5898240 | tf_op jit(solution)/shard_map/all_gather | solution.py:270
  332.4 215.4 %all-gather.18.cloned.1.call-start = ((), (), s32[]{:S(2)}) async-start(), calls=%async_computation.17 | async-start | bytes 3538944 | tf_op jit(solution)/shard_map/all_gather | solution.py:320
  332.4 73.2 %copy-start.94 = (f32[8,1,128]{2,1,0:T(1,128)}, f32[8,1,128]{2,1,0:T(1,128)S(1)}, u32[]{:S(2)}) copy-start(f32[8,1,128]{2,1,0:T(1,128)S(1)} %slice.33) | copy-start | bytes 12292
  333.1 80.0 %copy-start.95 = (pred[256]{0:T(512)(128)(4,1)}, pred[256]{0:T(512)(128)(4,1)S(1)}, u32[]{:S(2)}) copy-start(pred[256]{0:T(512)(128)(4,1)S(1)} %iota_compare_fusion.1) | copy-start | bytes 772
  333.5 76.8 %copy-start.59 = (f32[768]{0:T(1024)}, f32[768]{0:T(1024)S(1)}, u32[]{:S(2)}) copy-start(f32[768]{0:T(1024)S(1)} %convolution_reduce_fusion) | copy-start | bytes 9220
  487.1 299.0 %reduce-scatter.13.cloned.1.call-start = ((), (), s32[]{:S(2)}) async-start(), calls=%async_computation.14 | async-start | bytes 2433024 | tf_op jit(solution)/shard_map/reduce_scatter | solution.py:354
  494.3 304.5 %all-reduce.8.cloned.1.call-start = ((), (), s32[]{:S(2)}) async-start(), calls=%async_computation.18 | async-start | bytes 5505024 | tf_op jit(solution)/shard_map/psum | solution.py:360
  575.6 23.8 %copy-start.68 = (f32[8,33]{1,0:T(8,128)S(1)}, f32[8,33]{1,0:T(8,128)}, u32[]{:S(2)}) copy-start(f32[8,33]{1,0:T(8,128)} %copy-done.67) | copy-start | bytes 3172
  575.6 24.1 %copy-start.5 = (f32[8,33,2048]{2,1,0:T(8,128)S(1)}, f32[8,33,2048]{2,1,0:T(8,128)}, u32[]{:S(2)}) copy-start(f32[8,33,2048]{2,1,0:T(8,128)} %copy-done.4) | copy-start | bytes 6488068
  575.6 24.1 %copy-start.8 = (f32[8,33,2048]{2,1,0:T(8,128)S(1)}, f32[8,33,2048]{2,1,0:T(8,128)}, u32[]{:S(2)}) copy-start(f32[8,33,2048]{2,1,0:T(8,128)} %copy-done.7) | copy-start | bytes 6488068
  635.1 288.3 %reduce-scatter.11.cloned.1.call-start = ((), (), s32[]{:S(2)}) async-start(), calls=%async_computation.13 | async-start | bytes 7299072 | tf_op jit(solution)/shard_map/reduce_scatter | solution.py:353
  640.6 425.2 %reduce-scatter.17.cloned.1.call-start = ((), (), s32[]{:S(2)}) async-start(), calls=%async_computation.16 | async-start | bytes 9732096 | tf_op jit(solution)/shard_map/reduce_scatter | solution.py:356
  653.2 553.6 %reduce-scatter.15.cloned.1.call-start = ((), (), s32[]{:S(2)}) async-start(), calls=%async_computation.15 | async-start | bytes 9732096 | tf_op jit(solution)/shard_map/reduce_scatter | solution.py:355
  660.6 1380.0 %reduce-scatter.9.cloned.1.call-start = ((), (), s32[]{:S(2)}) async-start(), calls=%async_computation.12 | async-start | bytes 103809024 | tf_op jit(solution)/shard_map/reduce_scatter | solution.py:330
  742.5 1309.1 %copy-start.1 = (f32[128,2048]{1,0:T(8,128)S(1)}, f32[128,2048]{1,0:T(8,128)}, u32[]{:S(2)}) copy-start(f32[128,2048]{1,0:T(8,128)} %param.34) | copy-start | bytes 3145732
  798.9 1251.7 %copy-start.46 = (f32[2048,128]{1,0:T(8,128)S(1)}, f32[2048,128]{1,0:T(8,128)}, u32[]{:S(2)}) copy-start(f32[2048,128]{1,0:T(8,128)} %get-tuple-element.165) | copy-start | bytes 3145732
  (99 other events, 464.0 us)
Sparse Core Ops, SparseCore 0:
  11.8 278.2 all-gather.7
  330.0 72.5 reduce-scatter.6
  487.3 60.4 all-gather.17
  553.5 97.6 reduce-scatter.12
  659.7 139.0 all-reduce.7
  805.0 118.4 reduce-scatter.10
  931.0 134.7 reduce-scatter.16
  1072.3 134.5 reduce-scatter.14
  1215.0 825.6 reduce-scatter.8
Sparse Core Ops, SparseCore 1:
  331.9 28.7 all-gather.9
  362.2 17.3 all-gather.11
  381.0 37.3 all-gather.13
  419.9 37.3 all-gather.15
where the time goes:
time: 2070 us; the launch traced here: 2060 us
  waiting for transfers between devices  1670 us (81%)
  matrix products  245 us (12%)
  local copies, waits for them, and re-layouts  65.3 us (3%)
  blocking collectives  39.6 us (2%)
  other arithmetic  22.8 us (1%)
    reduce_scatter x1, waiting for transfers between devices, body(): lax.psum_scatter(contract_rows(d_kernel, band_low) * factor, ('band', 'to...  834 us
    all_gather x1, waiting for transfers between devices, body(): gen_full = lax.all_gather(gen_w, ('band', 'tok'), axis=0, tiled=True)  260 us
    reduce_scatter x1, waiting for transfers between devices, body(): lax.psum_scatter(grad_down, ('band', 'tok'), scatter_dimension=0, tiled=T...  142 us
    reduce_scatter x1, waiting for transfers between devices, body(): lax.psum_scatter(up_turned, ('band', 'tok'), scatter_dimension=0, tiled=T...  141 us
    reduce_scatter x1, waiting for transfers between devices, body(): lax.psum_scatter(qkv_turned, ('band', 'tok'), scatter_dimension=0, tiled=...  125 us
    reduce_scatter x1, waiting for transfers between devices, body(): lax.psum_scatter(product.reshape(own_images * slot_count * lax.axis_size(...  69.1 us
    dot_general x5, matrix products, contract_rows(): lax.dot_general(left_side, right_side, (((0,), (0,)), ((), ())), preferre...  66.2 us
    unnamed x232, local copies, waits for them, and re-layouts  54.6 us
  transfers between devices with their start and end apart: 13, of which 9 were waited for; matrix products, arithmetic and copies ran while one was open for 12% of the time, Pallas kernels for 0%

commit v1 on v0

--- a/solution.py
+++ b/solution.py
@@ -357,7 +357,7 @@
         lax.psum_scatter(gain_one, ("band", "tok"), scatter_dimension=0, tiled=True),
         lax.psum_scatter(gain_two, ("band", "tok"), scatter_dimension=0, tiled=True),
     )
-    hyper_sums = lax.psum(
+    extra = jax.lax.psum(
         (
             grad_token,
             grad_query,
@@ -370,8 +370,9 @@
             grad_second_gain,
             grad_gen_b,
         ),
-        ("band", "tok"),
-    )
+        axis_name="tok",
+    )
+    hyper_sums = jax.lax.psum(extra, axis_name="band")
     return (
         layer_out,
         pixel_grad,

time: 2070 us -> 2140 us (1.034)
  waiting for transfers between devices: 1670 us -> 1710 us
  blocking collectives: 39.6 us -> 67 us
    psum x1 -> x2, waiting for transfers between devices: 12.8 us -> 181 us  [the longest x1 123 us: body(): hyper_sums = jax.lax.psum(extra, axis_name='band')]
    reduce_scatter x1, waiting for transfers between devices: 125 us -> 0.01 us  [body(): lax.psum_scatter(qkv_turned, ('band', 'tok'), scatter_dimension=0, tiled=...]
    unnamed x0 -> x1, blocking collectives: none -> 39.5 us
    unnamed x232 -> x222, local copies, waits for them, and re-layouts: 54.6 us -> 51.5 us
  transfers between devices with their start and end apart: 13 -> 14, of which waited for: 9 -> 9; matrix products, arithmetic and copies ran while one was open for 12% -> 7% of each run, Pallas kernels for 0% -> 0%
where the time goes in v1:
time: 2140 us; the launch traced here: 2130 us
  waiting for transfers between devices  1710 us (80%)
  matrix products  242 us (11%)
  blocking collectives  67 us (3%)
  local copies, waits for them, and re-layouts  63.3 us (3%)
  other arithmetic  24 us (1%)
    reduce_scatter x1, waiting for transfers between devices, body(): lax.psum_scatter(contract_rows(d_kernel, band_low) * factor, ('band', 'to...  833 us
    all_gather x1, waiting for transfers between devices, body(): gen_full = lax.all_gather(gen_w, ('band', 'tok'), axis=0, tiled=True)  260 us
    reduce_scatter x1, waiting for transfers between devices, body(): lax.psum_scatter(up_turned, ('band', 'tok'), scatter_dimension=0, tiled=T...  142 us
    reduce_scatter x1, waiting for transfers between devices, body(): lax.psum_scatter(grad_down, ('band', 'tok'), scatter_dimension=0, tiled=T...  141 us
    psum x1, waiting for transfers between devices, body(): hyper_sums = jax.lax.psum(extra, axis_name='band')  123 us
    reduce_scatter x1, waiting for transfers between devices, body(): lax.psum_scatter(product.reshape(own_images * slot_count * lax.axis_size(...  69.1 us
    dot_general x5, matrix products, contract_rows(): lax.dot_general(left_side, right_side, (((0,), (0,)), ((), ())), preferre...  65.1 us
    psum x1, waiting for transfers between devices, body(): jax.lax.psum((grad_token, grad_query, grad_key, grad_value, grad_mix, gra...  58.2 us
  transfers between devices with their start and end apart: 14, of which 9 were waited for; matrix products, arithmetic and copies ran while one was open for 7% of the time, Pallas kernels for 0%

profile of v1, /device:TPU:0, one launch (start us, length us, event | category | flops | bytes accessed | tf_op | source)
XLA Modules:
  0.0 2129.2 jit_solution(15623021923495774067)
XLA Ops:
  30.0 260.0 %all-gather.8.cloned.1.call-done = bf16[196608,128]{1,0:T(8,128)(2,1)} async-done(((bf16[6144,128]{1,0:T(8,128)(2,1)}), bf16[196608,128]{1,0:T(8,128)(2,1)}) %all-gather.8.cloned.1.call-update) | async-done | bytes 50331664 | tf_op jit(solution)/shard_map/all_gather | solution.py:284
  290.0 25.8 %fusion.1 = bf16[32,196608]{1,0:T(8,128)(2,1)} fusion(bf16[32,128]{1,0:T(8,128)(2,1)S(1)} %bitcast.310, bf16[196608,128]{1,0:T(8,128)(2,1)} %all-gather.8.cloned.1.call-done), kind=kOutput, calls=%fused_computation.3 | convolution fusion | flops 1623195648 | bytes 62922752 | tf_op jit(solution)/shard_map/dot_general | solution.py:93
  315.9 8.2 copy.211
  333.4 69.1 %reduce-scatter.7.cloned.1.call-done = bf16[256,768]{1,0:T(8,128)(2,1)} async-done(((bf16[2048,768]{1,0:T(8,128)(2,1)}), bf16[256,768]{1,0:T(8,128)(2,1)}) %reduce-scatter.7.cloned.1.call-update) | async-done | bytes 393232 | tf_op jit(solution)/shard_map/reduce_scatter | solution.py:291
  427.2 30.0 %all-gather.16.cloned.1.call-done = bf16[3072,768]{1,0:T(8,128)(2,1)} async-done(((bf16[768,768]{1,0:T(8,128)(2,1)}), bf16[3072,768]{1,0:T(8,128)(2,1)}) %all-gather.16.cloned.1.call-update) | async-done | bytes 4718608 | tf_op jit(solution)/shard_map/all_gather | solution.py:270
  457.2 11.0 add_convert_fusion
  493.5 54.4 %all-gather.18.cloned.1.call-done = bf16[2048,768]{1,0:T(8,128)(2,1)} async-done(((bf16[256,768]{1,0:T(8,128)(2,1)}), bf16[2048,768]{1,0:T(8,128)(2,1)}) %all-gather.18.cloned.1.call-update) | async-done | bytes 3145744 | tf_op jit(solution)/shard_map/all_gather | solution.py:320
  547.9 11.1 convert_bitcast_fusion
  559.0 16.7 copy.212
  575.7 22.2 %convolution_multiply_fusion.5 = f32[32,128]{1,0:T(8,128)S(1)} fusion(bf16[32,196608]{1,0:T(8,128)(2,1)} %bitcast.272, bf16[196608,128]{1,0:T(8,128)(2,1)} %all-gather.8.cloned.1.call-done), kind=kOutput, calls=%fused_computation.123 | convolution fusion | flops 1610616832 | bytes 62930944 | tf_op jit(solution)/shard_map/dot_general | solution.py:329
  641.9 58.2 %all-reduce.14.cloned.1.call-done = (f32[128,768]{1,0:T(8,128)}, f32[128,128]{1,0:T(8,128)}, f32[128,128]{1,0:T(8,128)}, f32[128,128]{1,0:T(8,128)}, f32[128,128...) async-done(((f32[128,768]{1,0:T(8,128)}, f32[128,128]{1,0:T(8,128)}, f32[128,128]{1,0:T(8,128)}, f32[128,128]{1,0:T(8,128)}, f32[128,128]{1,0:T(8,128)}, ...) | async-done | bytes 2752528 | tf_op jit(solution)/shard_map/psum | solution.py:360
  700.2 11.6 fusion.34
  712.5 6.8 fusion.194
  720.0 39.4 %convolution_multiply_fusion = f32[196608,128]{1,0:T(8,128)} fusion(bf16[32,196608]{1,0:T(8,128)(2,1)} %bitcast.273, bf16[32,128]{1,0:T(8,128)(2,1)S(1)} %bitcast.311), kind=kOutput, calls=%fused_computation.1 | convolution fusion | flops 1635778560 | bytes 113254400 | tf_op jit(solution)/shard_map/dot_general | solution.py:87
  764.3 39.5 %all-reduce.4 = (f32[768]{0:T(1024)S(1)}, f32[768]{0:T(1024)S(1)}) all-reduce(f32[768]{0:T(1024)S(1)} %copy-done.100, f32[768]{0:T(1024)S(1)} %copy-done.99), channel_id=9, replica_groups=mesh['band'=8,'tok'=4] {'band','tok'}, use_global_device_ids=true, to_apply=%region_60.61.clone | all-reduce | flops 1536 | bytes 12288
  809.1 13.5 fusion.65
  822.6 11.3 convert_bitcast_fusion.1
  834.0 6.6 copy.179
  844.3 7.1 all-reduce.7
  851.4 20.5 all-reduce.5
  871.8 122.8 %all-reduce.12.cloned.1.call-done = (f32[128,768]{1,0:T(8,128)}, f32[128,128]{1,0:T(8,128)}, f32[128,128]{1,0:T(8,128)}, f32[128,128]{1,0:T(8,128)}, f32[128,128...) async-done(((f32[128,768]{1,0:T(8,128)}, f32[128,128]{1,0:T(8,128)}, f32[128,128]{1,0:T(8,128)}, f32[128,128]{1,0:T(8,128)}, f32[128,128]{1,0:T(8,128)}, ...) | async-done | bytes 2752528 | tf_op jit(solution)/shard_map/psum | solution.py:375
  994.6 140.8 %reduce-scatter.17.cloned.1.call-done = f32[96,768]{1,0:T(8,128)} async-done(((f32[3072,768]{1,0:T(8,128)}), f32[96,768]{1,0:T(8,128)}) %reduce-scatter.17.cloned.1.call-update) | async-done | bytes 294928 | tf_op jit(solution)/shard_map/reduce_scatter | solution.py:356
  1135.4 142.3 %reduce-scatter.15.cloned.1.call-done = f32[96,768]{1,0:T(8,128)} async-done(((f32[3072,768]{1,0:T(8,128)}), f32[96,768]{1,0:T(8,128)}) %reduce-scatter.15.cloned.1.call-update) | async-done | bytes 294928 | tf_op jit(solution)/shard_map/reduce_scatter | solution.py:355
  1277.7 832.7 %reduce-scatter.9.cloned.1.call-done = f32[6144,128]{1,0:T(8,128)} async-done(((f32[196608,128]{1,0:T(8,128)}), f32[6144,128]{1,0:T(8,128)}) %reduce-scatter.9.cloned.1.call-update) | async-done | bytes 3145744 | tf_op jit(solution)/shard_map/reduce_scatter | solution.py:330
  (368 shorter events, 149.6 us)
Async XLA Ops:
  8.1 282.0 %all-gather.8.cloned.1.call-start = ((), (), s32[]{:S(2)}) async-start(), calls=%async_computation.6 | async-start | bytes 51904512 | tf_op jit(solution)/shard_map/all_gather | solution.py:284
  8.8 393.7 %reduce-scatter.7.cloned.1.call-start = ((), (), s32[]{:S(2)}) async-start(), calls=%async_computation.7 | async-start | bytes 3538944 | tf_op jit(solution)/shard_map/reduce_scatter | solution.py:291
  29.8 286.1 %copy-start.63 = (f32[8,33]{1,0:T(8,128)}, f32[8,33]{1,0:T(8,128)S(1)}, u32[]{:S(2)}) copy-start(f32[8,33]{1,0:T(8,128)S(1)} %multiply_reduce_fusion.14) | copy-start | bytes 3172
  30.0 285.8 %copy-start.53 = (bf16[8,4,128]{2,1,0:T(4,128)(2,1)}, bf16[8,4,128]{2,1,0:T(4,128)(2,1)S(1)}, u32[]{:S(2)}) copy-start(bf16[8,4,128]{2,1,0:T(4,128)(2,1)S(1)} %dynamic-slice_convert_fusion) | copy-start | bytes 24580
  329.8 76.0 %all-gather.10.cloned.1.call-start = ((), (), s32[]{:S(2)}) async-start(), calls=%async_computation.8 | async-start | bytes 4423680 | tf_op jit(solution)/shard_map/all_gather | solution.py:267
  330.4 75.5 %copy-start.65 = (f32[768]{0:T(1024)S(1)}, f32[768]{0:T(1024)}, u32[]{:S(2)}) copy-start(f32[768]{0:T(1024)} %param.42) | copy-start | bytes 9220
  330.4 87.6 %all-gather.12.cloned.1.call-start = ((), (), s32[]{:S(2)}) async-start(), calls=%async_computation.9 | async-start | bytes 1474560 | tf_op jit(solution)/shard_map/all_gather | solution.py:268
  331.0 90.7 %all-gather.14.cloned.1.call-start = ((), (), s32[]{:S(2)}) async-start(), calls=%async_computation.10 | async-start | bytes 5898240 | tf_op jit(solution)/shard_map/all_gather | solution.py:269
  331.6 125.6 %all-gather.16.cloned.1.call-start = ((), (), s32[]{:S(2)}) async-start(), calls=%async_computation.11 | async-start | bytes 5898240 | tf_op jit(solution)/shard_map/all_gather | solution.py:270
  332.3 215.6 %all-gather.18.cloned.1.call-start = ((), (), s32[]{:S(2)}) async-start(), calls=%async_computation.17 | async-start | bytes 3538944 | tf_op jit(solution)/shard_map/all_gather | solution.py:320
  332.4 73.1 %copy-start.89 = (f32[8,1,128]{2,1,0:T(1,128)}, f32[8,1,128]{2,1,0:T(1,128)S(1)}, u32[]{:S(2)}) copy-start(f32[8,1,128]{2,1,0:T(1,128)S(1)} %slice.33) | copy-start | bytes 12292
  333.1 79.6 %copy-start.90 = (pred[256]{0:T(512)(128)(4,1)}, pred[256]{0:T(512)(128)(4,1)S(1)}, u32[]{:S(2)}) copy-start(pred[256]{0:T(512)(128)(4,1)S(1)} %iota_compare_fusion.1) | copy-start | bytes 772
  333.4 76.7 %copy-start.55 = (f32[768]{0:T(1024)}, f32[768]{0:T(1024)S(1)}, u32[]{:S(2)}) copy-start(f32[768]{0:T(1024)S(1)} %convolution_reduce_fusion) | copy-start | bytes 9220
  487.3 212.8 %all-reduce.14.cloned.1.call-start = ((), (), s32[]{:S(2)}) async-start(), calls=%async_computation.19 | async-start | bytes 5505024 | tf_op jit(solution)/shard_map/psum | solution.py:360
  634.2 237.6 %reduce-scatter.13.cloned.1.call-start = ((), (), s32[]{:S(2)}) async-start(), calls=%async_computation.14 | async-start | bytes 2433024 | tf_op jit(solution)/shard_map/reduce_scatter | solution.py:354
  636.2 235.6 %reduce-scatter.11.cloned.1.call-start = ((), (), s32[]{:S(2)}) async-start(), calls=%async_computation.13 | async-start | bytes 7299072 | tf_op jit(solution)/shard_map/reduce_scatter | solution.py:353
  641.8 58.3 %copy-start.39 = (bf16[1,1,256,768]{3,2,1,0:T(8,128)(2,1)S(1)}, bf16[1,1,256,768]{3,2,1,0:T(8,128)(2,1)}, u32[]{:S(2)}) copy-start(bf16[1,1,256,768]{3,2,1,0:T(8,128)(2,1)} %param.26) | copy-start | bytes 1179652
  641.8 58.3 %copy-start.93 = (pred[256]{0:T(512)(128)(4,1)S(1)}, pred[256]{0:T(512)(128)(4,1)}, u32[]{:S(2)}) copy-start(pred[256]{0:T(512)(128)(4,1)} %copy-done.90) | copy-start | bytes 772
  641.9 352.7 %all-reduce.12.cloned.1.call-start = ((), (), s32[]{:S(2)}) async-start(), calls=%async_computation.18 | async-start | bytes 5505024 | tf_op jit(solution)/shard_map/psum | solution.py:375
  700.1 435.3 %reduce-scatter.17.cloned.1.call-start = ((), (), s32[]{:S(2)}) async-start(), calls=%async_computation.16 | async-start | bytes 9732096 | tf_op jit(solution)/shard_map/reduce_scatter | solution.py:356
  711.8 565.9 %reduce-scatter.15.cloned.1.call-start = ((), (), s32[]{:S(2)}) async-start(), calls=%async_computation.15 | async-start | bytes 9732096 | tf_op jit(solution)/shard_map/reduce_scatter | solution.py:355
  719.3 1391.1 %reduce-scatter.9.cloned.1.call-start = ((), (), s32[]{:S(2)}) async-start(), calls=%async_computation.12 | async-start | bytes 103809024 | tf_op jit(solution)/shard_map/reduce_scatter | solution.py:330
  841.5 1279.8 %copy-start.1 = (f32[128,2048]{1,0:T(8,128)S(1)}, f32[128,2048]{1,0:T(8,128)}, u32[]{:S(2)}) copy-start(f32[128,2048]{1,0:T(8,128)} %param.34) | copy-start | bytes 3145732
  994.6 1125.8 %copy-start.41 = (f32[2048,128]{1,0:T(8,128)S(1)}, f32[2048,128]{1,0:T(8,128)}, u32[]{:S(2)}) copy-start(f32[2048,128]{1,0:T(8,128)} %get-tuple-element.175) | copy-start | bytes 3145732
  (95 other events, 487.3 us)
Sparse Core Ops, SparseCore 0:
  11.8 278.2 all-gather.7
  330.0 72.5 reduce-scatter.6
  487.4 60.4 all-gather.17
  640.6 103.6 reduce-scatter.12
  751.4 117.9 reduce-scatter.10
  873.8 120.7 all-reduce.11
  1001.1 134.3 reduce-scatter.16
  1142.9 134.7 reduce-scatter.14
  1284.7 825.6 reduce-scatter.8
Sparse Core Ops, SparseCore 1:
  331.9 28.7 all-gather.9
  362.1 17.3 all-gather.11
  380.9 37.3 all-gather.13
  419.9 37.3 all-gather.15
  634.3 65.8 all-reduce.13
